TPU v7x, 32 devices: a whole 2x2x4 slice. The times are simulated.
32 devices in a mesh: seg: 4 (over z), slab: 8 (over y, x, core).
Axes of the slice: x: 2, y: 2, z: 4, core: 2. Of those that a mesh axis runs over, the one named last changes fastest.
Arguments:
- checkpoints: float32 [4, 32, 256, 512], P('seg', 'slab'), may hold values from 0 to 1
- control: float32 [4, 32, 256, 512], P('seg', 'slab'), may hold values from -4 to 4
- rate: float32 [32, 256, 512], P('slab'), may hold values from 0.25 to 2.5
- target: float32 [32, 256, 512], P('slab'), may hold values from 0 to 1
Outputs:
- new_checkpoints: float32 [4, 32, 256, 512], P('seg', 'slab')
- new_control: float32 [4, 32, 256, 512], P('seg', 'slab')
All inputs are finite; a program needn't handle non-finite values.
Results may differ from a plain program's by a relative error of at most 0.00002.
Values sent between devices are 32-bit elements; how exact they have to be, the bound alone decides.
A program may use at most 128 MiB of HBM per device.

v0:
```python
import jax
import jax.numpy as jnp
from jax import lax
from jax.sharding import PartitionSpec as P

STEPS = 2


def extended_2(block, sides, width):
    for axis, dim in sides:
        count = lax.axis_size(axis)
        forward = [(i, i + 1) for i in range(count - 1)]
        backward = [(target, source) for source, target in forward]
        low = lax.ppermute(
            lax.slice_in_dim(block, block.shape[dim] - width, None, axis=dim), axis, forward
        )
        high = lax.ppermute(lax.slice_in_dim(block, 0, width, axis=dim), axis, backward)
        block = jnp.concatenate([low, block, high], axis=dim)
    return block


def passed_along(block, axis, distance):
    devices = range(lax.axis_size(axis))
    route = [(i - distance, i) for i in devices if i - distance in devices]
    return lax.ppermute(block, axis, route)


def planar(extended):
    inner = extended[1:-1]
    padded = jnp.pad(inner, ((0, 0), (1, 1), (1, 1)))
    beside = extended[2:] + extended[:-2]
    beside = beside + padded[:, 2:, 1:-1] + padded[:, :-2, 1:-1]
    beside = beside + padded[:, 1:-1, 2:] + padded[:, 1:-1, :-2]
    return beside - 6.0 * inner


def per_device(checkpoints, control, rate, target):
    start = checkpoints[0]
    source = control[0]
    seg_count = lax.axis_size("seg")
    slab_count = lax.axis_size("slab")
    seg_index = lax.axis_index("seg")
    is_last = seg_index == seg_count - 1
    is_first = seg_index == 0
    path = [start]
    state = start
    for t in range(STEPS):
        extended = extended_2(state, (("slab", 0),), 1)
        state = state + 0.1 * (planar(extended) + rate * state * (1.0 - state) + source)
        path.append(state)
    arriving = passed_along(state, "seg", 1)
    prior = jnp.where(is_first, 0.0, arriving - start)
    returned = passed_along(prior, "seg", -1)
    defect = jnp.where(is_last, state - target, returned)
    costate = defect
    summed = jnp.zeros_like(start)
    for t in range(STEPS - 1, -1, -1):
        summed = summed + costate
        extended = extended_2(costate, (("slab", 0),), 1)
        costate = costate + 0.1 * (planar(extended) + rate * (1.0 - 2.0 * path[t]) * costate)
    grad_control = 0.1 * summed
    grad_start = costate - prior
    local_sum = jnp.sum(grad_control * grad_control) + jnp.sum(grad_start * grad_start)
    squared = lax.psum(local_sum, ("seg", "slab"))
    count = 2.0 * seg_count * slab_count * start.size
    scale = 0.5 / jnp.sqrt(squared / count + 1e-06)
    return ((start - scale * grad_start)[None], (source - scale * grad_control)[None])


def solution(mesh):
    return jax.shard_map(
        per_device,
        mesh=mesh,
        in_specs=(
            P("seg", "slab", None, None),
            P("seg", "slab", None, None),
            P("slab", None, None),
            P("slab", None, None),
        ),
        out_specs=(P("seg", "slab", None, None), P("seg", "slab", None, None)),
        check_vma=False,
    )
```

profile of v0, /device:TPU:0, one launch (start us, length us, event | category | flops | bytes accessed | tf_op | source)
XLA Modules:
  0.0 238.9 jit_solution(3826204480665517907)
XLA Ops:
  0.6 0.0 copy-start
  0.6 1.4 slice_bitcast_fusion.1
  2.1 1.3 collective-permute-start
  3.4 3.1 %collective-permute-start.1 = (f32[1,256,512]{2,1,0:T(8,128)S(1)}, f32[1,256,512]{2,1,0:T(8,128)S(1)}, u32[]{:S(2)}, u32[]{:S(2)}) collective-permute-start(f32[1,256,512]{2,1,0:T(8,128)S(1)} %get-tuple-element.14), channel_id=1, source_target_pairs={{0,1},{1,2},{2,3},{3,4},{4,5},{5,6},{6,7},{8,9},{9,10},{10,11},{11... | collective-permute-start | bytes 1572872 | tf_op jit(solution)/shard_map/ppermute | solution.py:14
  6.4 0.0 collective-permute-done
  6.4 1.5 collective-permute-done.1
  7.9 0.0 copy-done
  7.9 0.0 copy-start.5
  7.9 4.3 %fusion.8 = f32[4,256,512]{2,1,0:T(8,128)S(1)} fusion(f32[4,256,512]{2,1,0:T(8,128)S(1)} %bitcast.19, f32[1,256,512]{2,1,0:T(8,128)S(1)} %collective-permute-done.1, f32[1,256,512]{2,1,0:T(8,128)S(1)} %collective-permute-done, f32[1,4,256,512]{3,2,1,0:T(8,128)} %param.5, f32[4,256,512]{2,1,0:T(8,128)} %param.6), kind=kLoop, calls=%fused_computation.24 | loop fusion | flops 8388608 | bytes 9437184 | tf_op jit(solution)/shard_map/add | solution.py:49
  12.2 0.0 copy-start.3
  12.2 0.0 copy-start.1
  12.2 0.1 fusion.46
  12.3 1.6 collective-permute-start.2
  13.8 10.4 %collective-permute-start.3 = (f32[1,256,512]{2,1,0:T(8,128)S(1)}, f32[1,256,512]{2,1,0:T(8,128)S(1)}, u32[]{:S(2)}, u32[]{:S(2)}) collective-permute-start(f32[1,256,512]{2,1,0:T(8,128)S(1)} %get-tuple-element.12), channel_id=1, source_target_pairs={{0,1},{1,2},{2,3},{3,4},{4,5},{5,6},{6,7},{8,9},{9,10},{10,11},{11... | collective-permute-start | bytes 1572872 | tf_op jit(solution)/shard_map/ppermute | solution.py:14
  24.3 0.0 collective-permute-done.2
  24.3 1.5 collective-permute-done.3
  25.7 0.0 copy-done.5
  25.7 0.0 copy-done.1
  25.7 3.6 %fusion.17 = f32[4,256,512]{2,1,0:T(8,128)} fusion(f32[4,256,512]{2,1,0:T(8,128)S(1)} %fusion.8, f32[1,256,512]{2,1,0:T(8,128)S(1)} %collective-permute-done.3, f32[1,256,512]{2,1,0:T(8,128)S(1)} %collective-permute-done.2, f32[1,4,256,512]{3,2,1,0:T(8,128)S(1)} %copy-done.5, f32[4,256,512]{2,1,0:T(8,128)S(1)} %copy-done.1), kind=kLoop, calls=%fused_computation.33 | loop fusion | flops 8388608 | bytes 9437184 | tf_op jit(solution)/shard_map/add | solution.py:49
  29.3 0.0 copy-done.3
  29.3 4.8 %collective-permute-start.4 = (f32[4,256,512]{2,1,0:T(8,128)}, f32[4,256,512]{2,1,0:T(8,128)}, u32[]{:S(2)}, u32[]{:S(2)}) collective-permute-start(f32[4,256,512]{2,1,0:T(8,128)} %fusion.17), channel_id=1, source_target_pairs={{0,8},{8,16},{16,24},{1,9},{9,17},{17,25},{2,10},{10,18},{18,26},{... | collective-permute-start | bytes 6291464 | tf_op jit(solution)/shard_map/ppermute | solution.py:25
  34.1 39.5 %collective-permute-done.4 = f32[4,256,512]{2,1,0:T(8,128)} collective-permute-done((f32[4,256,512]{2,1,0:T(8,128)}, f32[4,256,512]{2,1,0:T(8,128)}, u32[]{:S(2)}, u32[]{:S(2)}) %collective-permute-start.4) | collective-permute-done | bytes 2097184 | tf_op jit(solution)/shard_map/ppermute | solution.py:25
  73.6 3.4 %subtract_select_fusion = f32[4,256,512]{2,1,0:T(8,128)} fusion(f32[4,256,512]{2,1,0:T(8,128)} %collective-permute-done.4, pred[]{:T(512)S(6)} %eq.7, f32[1,4,256,512]{3,2,1,0:T(8,128)S(1)} %copy-done), kind=kLoop, calls=%fused_computation.68 | loop fusion | flops 1048576 | bytes 6291457 | tf_op jit(solution)/shard_map/jit(_where)/select_n | solution.py:52
  77.0 1.3 collective-permute-start.5
  78.3 45.2 %collective-permute-done.5 = f32[4,256,512]{2,1,0:T(8,128)} collective-permute-done((f32[4,256,512]{2,1,0:T(8,128)}, f32[4,256,512]{2,1,0:T(8,128)}, u32[]{:S(2)}, u32[]{:S(2)}) %collective-permute-start.5) | collective-permute-done | bytes 2097184 | tf_op jit(solution)/shard_map/ppermute | solution.py:25
  123.5 0.0 copy-start.4
  123.5 0.0 copy-start.6
  123.5 3.8 %subtract_select_fusion.1 = f32[4,256,512]{2,1,0:T(8,128)S(1)} fusion(f32[4,256,512]{2,1,0:T(8,128)} %collective-permute-done.5, f32[4,256,512]{2,1,0:T(8,128)} %fusion.17, f32[4,256,512]{2,1,0:T(8,128)} %param.7, pred[]{:T(512)S(6)} %eq.6), kind=kLoop, calls=%fused_computation.69 | loop fusion | flops 1048576 | bytes 8388609 | tf_op jit(solution)/shard_map/jit(_where)/select_n | solution.py:54
  127.3 0.0 copy-start.2
  127.3 0.1 fusion.45
  127.4 1.4 collective-permute-start.6
  128.8 7.1 %collective-permute-start.7 = (f32[1,256,512]{2,1,0:T(8,128)S(1)}, f32[1,256,512]{2,1,0:T(8,128)S(1)}, u32[]{:S(2)}, u32[]{:S(2)}) collective-permute-start(f32[1,256,512]{2,1,0:T(8,128)S(1)} %get-tuple-element.10), channel_id=1, source_target_pairs={{0,1},{1,2},{2,3},{3,4},{4,5},{5,6},{6,7},{8,9},{9,10},{10,11},{11... | collective-permute-start | bytes 1572872 | tf_op jit(solution)/shard_map/ppermute | solution.py:14
  135.9 0.0 collective-permute-done.6
  135.9 1.5 collective-permute-done.7
  137.4 0.0 copy-done.4
  137.4 0.0 copy-done.6
  137.4 0.0 copy-done.2
  137.4 6.1 %multiply_reduce_fusion.1 = (f32[]{:T(128)}, f32[4,256,512]{2,1,0:T(8,128)}, f32[4,256,512]{2,1,0:T(8,128)S(1)}) fusion(f32[4,256,512]{2,1,0:T(8,128)} %collective-permute-done.5, f32[4,256,512]{2,1,0:T(8,128)} %fusion.17, f32[4,256,512]{2,1,0:T(8,128)S(1)} %copy-done.6, pred[]{:T(512)S(6)} %eq.6, f32[4,256,512]{2,1,0:T(8,128)S(1)} %subtract_select_fusion.1, ...), kind=kLoop, calls=%fused_computation.67 | loop fusion | flops 11534335 | bytes 17825796 | tf_op jit(solution)/shard_map/reduce_sum | solution.py:63
  143.5 0.1 fusion.44
  143.5 1.3 collective-permute-start.8
  144.8 15.5 %collective-permute-start.9 = (f32[1,256,512]{2,1,0:T(8,128)S(1)}, f32[1,256,512]{2,1,0:T(8,128)S(1)}, u32[]{:S(2)}, u32[]{:S(2)}) collective-permute-start(f32[1,256,512]{2,1,0:T(8,128)S(1)} %get-tuple-element.8), channel_id=1, source_target_pairs={{0,1},{1,2},{2,3},{3,4},{4,5},{5,6},{6,7},{8,9},{9,10},{10,11},{11... | collective-permute-start | bytes 1572872 | tf_op jit(solution)/shard_map/ppermute | solution.py:14
  160.3 0.0 collective-permute-done.8
  160.3 1.5 collective-permute-done.9
  161.8 5.4 %multiply_reduce_fusion = (f32[]{:T(128)}, f32[4,256,512]{2,1,0:T(8,128)}) fusion(f32[4,256,512]{2,1,0:T(8,128)} %subtract_select_fusion, f32[4,256,512]{2,1,0:T(8,128)S(1)} %get-tuple-element.6, f32[4,256,512]{2,1,0:T(8,128)S(1)} %copy-done.2, f32[1,4,256,512]{3,2,1,0:T(8,128)S(1)} %copy-done, f32[1,256,512]{2,1,0:T(8,128)S(1)} %collective-permute-done.9, ...), kind=kLoop, calls=%fused_computation.66 | loop fusion | flops 9961471 | bytes 11534340 | tf_op jit(solution)/shard_map/reduce_sum | solution.py:63
  168.5 63.9 %psum.7 = f32[]{:T(128)} all-reduce(f32[]{:T(128)S(6)} %add.140), channel_id=1, replica_groups=mesh['seg'=4,'slab'=8] {'seg','slab'}, use_global_device_ids=true, to_apply=%region_2.3 | all-reduce | flops 1 | bytes 8 | tf_op jit(solution)/shard_map/psum | solution.py:64
  233.0 5.9 %fusion.39 = (f32[1,4,256,512]{3,2,1,0:T(8,128)}, f32[1,4,256,512]{3,2,1,0:T(8,128)}) fusion(f32[1,4,256,512]{3,2,1,0:T(8,128)} %param.5, f32[4,256,512]{2,1,0:T(8,128)} %get-tuple-element.5, f32[]{:T(128)S(6)} %mul.100, f32[4,256,512]{2,1,0:T(8,128)} %get-tuple-element.3, f32[]{:T(128)S(6)} %div.7, f32[1,4,256,512]{3,2,1,0:T(8,128)S(1)} %copy-done), kind=kLoop, calls=%fused_computation.64 | loop fusion | flops 2097152 | bytes 12582920 | tf_op jit(solution)/shard_map/broadcast_in_dim | solution.py:67
Async XLA Ops:
  0.6 7.3 %copy-start = (f32[1,4,256,512]{3,2,1,0:T(8,128)S(1)}, f32[1,4,256,512]{3,2,1,0:T(8,128)}, u32[]{:S(2)}) copy-start(f32[1,4,256,512]{3,2,1,0:T(8,128)} %param.4) | copy-start | bytes 6291460
  2.1 4.4 %collective-permute-start = (f32[1,256,512]{2,1,0:T(8,128)S(1)}, f32[1,256,512]{2,1,0:T(8,128)S(1)}, u32[]{:S(2)}, u32[]{:S(2)}) collective-permute-start(f32[1,256,512]{2,1,0:T(8,128)S(1)} %get-tuple-element.13), channel_id=1, source_target_pairs={{1,0},{2,1},{3,2},{4,3},{5,4},{6,5},{7,6},{9,8},{10,9},{11,10},{12... | collective-permute-start | bytes 1572872 | tf_op jit(solution)/shard_map/ppermute | solution.py:17
  3.4 4.6 %collective-permute-start.1 = (f32[1,256,512]{2,1,0:T(8,128)S(1)}, f32[1,256,512]{2,1,0:T(8,128)S(1)}, u32[]{:S(2)}, u32[]{:S(2)}) collective-permute-start(f32[1,256,512]{2,1,0:T(8,128)S(1)} %get-tuple-element.14), channel_id=1, source_target_pairs={{0,1},{1,2},{2,3},{3,4},{4,5},{5,6},{6,7},{8,9},{9,10},{10,11},{11... | collective-permute-start | bytes 1572872 | tf_op jit(solution)/shard_map/ppermute | solution.py:14
  7.9 17.8 %copy-start.5 = (f32[1,4,256,512]{3,2,1,0:T(8,128)S(1)}, f32[1,4,256,512]{3,2,1,0:T(8,128)}, u32[]{:S(2)}) copy-start(f32[1,4,256,512]{3,2,1,0:T(8,128)} %param.5) | copy-start | bytes 6291460
  12.2 17.1 %copy-start.3 = (f32[4,256,512]{2,1,0:T(8,128)}, f32[4,256,512]{2,1,0:T(8,128)S(1)}, u32[]{:S(2)}) copy-start(f32[4,256,512]{2,1,0:T(8,128)S(1)} %fusion.8) | copy-start | bytes 6291460
  12.2 13.6 %copy-start.1 = (f32[4,256,512]{2,1,0:T(8,128)S(1)}, f32[4,256,512]{2,1,0:T(8,128)}, u32[]{:S(2)}) copy-start(f32[4,256,512]{2,1,0:T(8,128)} %param.6) | copy-start | bytes 6291460
  12.3 12.0 %collective-permute-start.2 = (f32[1,256,512]{2,1,0:T(8,128)S(1)}, f32[1,256,512]{2,1,0:T(8,128)S(1)}, u32[]{:S(2)}, u32[]{:S(2)}) collective-permute-start(f32[1,256,512]{2,1,0:T(8,128)S(1)} %get-tuple-element.11), channel_id=1, source_target_pairs={{1,0},{2,1},{3,2},{4,3},{5,4},{6,5},{7,6},{9,8},{10,9},{11,10},{12... | collective-permute-start | bytes 1572872 | tf_op jit(solution)/shard_map/ppermute | solution.py:17
  13.8 11.9 %collective-permute-start.3 = (f32[1,256,512]{2,1,0:T(8,128)S(1)}, f32[1,256,512]{2,1,0:T(8,128)S(1)}, u32[]{:S(2)}, u32[]{:S(2)}) collective-permute-start(f32[1,256,512]{2,1,0:T(8,128)S(1)} %get-tuple-element.12), channel_id=1, source_target_pairs={{0,1},{1,2},{2,3},{3,4},{4,5},{5,6},{6,7},{8,9},{9,10},{10,11},{11... | collective-permute-start | bytes 1572872 | tf_op jit(solution)/shard_map/ppermute | solution.py:14
  29.3 44.3 %collective-permute-start.4 = (f32[4,256,512]{2,1,0:T(8,128)}, f32[4,256,512]{2,1,0:T(8,128)}, u32[]{:S(2)}, u32[]{:S(2)}) collective-permute-start(f32[4,256,512]{2,1,0:T(8,128)} %fusion.17), channel_id=1, source_target_pairs={{0,8},{8,16},{16,24},{1,9},{9,17},{17,25},{2,10},{10,18},{18,26},{... | collective-permute-start | bytes 6291464 | tf_op jit(solution)/shard_map/ppermute | solution.py:25
  77.0 46.5 %collective-permute-start.5 = (f32[4,256,512]{2,1,0:T(8,128)}, f32[4,256,512]{2,1,0:T(8,128)}, u32[]{:S(2)}, u32[]{:S(2)}) collective-permute-start(f32[4,256,512]{2,1,0:T(8,128)} %subtract_select_fusion), channel_id=1, source_target_pairs={{8,0},{16,8},{24,16},{9,1},{17,9},{25,17},{10,2},{18,10},{26,18},{... | collective-permute-start | bytes 6291464 | tf_op jit(solution)/shard_map/ppermute | solution.py:25
  123.5 13.9 %copy-start.4 = (f32[4,256,512]{2,1,0:T(8,128)S(1)}, f32[4,256,512]{2,1,0:T(8,128)}, u32[]{:S(2)}) copy-start(f32[4,256,512]{2,1,0:T(8,128)} %copy-done.3) | copy-start | bytes 6291460
  123.5 13.9 %copy-start.6 = (f32[4,256,512]{2,1,0:T(8,128)S(1)}, f32[4,256,512]{2,1,0:T(8,128)}, u32[]{:S(2)}) copy-start(f32[4,256,512]{2,1,0:T(8,128)} %param.7) | copy-start | bytes 6291460
  127.3 10.1 %copy-start.2 = (f32[4,256,512]{2,1,0:T(8,128)S(1)}, f32[4,256,512]{2,1,0:T(8,128)}, u32[]{:S(2)}) copy-start(f32[4,256,512]{2,1,0:T(8,128)} %param.6) | copy-start | bytes 6291460
  127.4 8.5 %collective-permute-start.6 = (f32[1,256,512]{2,1,0:T(8,128)S(1)}, f32[1,256,512]{2,1,0:T(8,128)S(1)}, u32[]{:S(2)}, u32[]{:S(2)}) collective-permute-start(f32[1,256,512]{2,1,0:T(8,128)S(1)} %get-tuple-element.9), channel_id=1, source_target_pairs={{1,0},{2,1},{3,2},{4,3},{5,4},{6,5},{7,6},{9,8},{10,9},{11,10},{12... | collective-permute-start | bytes 1572872 | tf_op jit(solution)/shard_map/ppermute | solution.py:17
  128.8 8.6 %collective-permute-start.7 = (f32[1,256,512]{2,1,0:T(8,128)S(1)}, f32[1,256,512]{2,1,0:T(8,128)S(1)}, u32[]{:S(2)}, u32[]{:S(2)}) collective-permute-start(f32[1,256,512]{2,1,0:T(8,128)S(1)} %get-tuple-element.10), channel_id=1, source_target_pairs={{0,1},{1,2},{2,3},{3,4},{4,5},{5,6},{6,7},{8,9},{9,10},{10,11},{11... | collective-permute-start | bytes 1572872 | tf_op jit(solution)/shard_map/ppermute | solution.py:14
  143.5 16.8 %collective-permute-start.8 = (f32[1,256,512]{2,1,0:T(8,128)S(1)}, f32[1,256,512]{2,1,0:T(8,128)S(1)}, u32[]{:S(2)}, u32[]{:S(2)}) collective-permute-start(f32[1,256,512]{2,1,0:T(8,128)S(1)} %get-tuple-element.7), channel_id=1, source_target_pairs={{1,0},{2,1},{3,2},{4,3},{5,4},{6,5},{7,6},{9,8},{10,9},{11,10},{12... | collective-permute-start | bytes 1572872 | tf_op jit(solution)/shard_map/ppermute | solution.py:17
  144.8 16.9 %collective-permute-start.9 = (f32[1,256,512]{2,1,0:T(8,128)S(1)}, f32[1,256,512]{2,1,0:T(8,128)S(1)}, u32[]{:S(2)}, u32[]{:S(2)}) collective-permute-start(f32[1,256,512]{2,1,0:T(8,128)S(1)} %get-tuple-element.8), channel_id=1, source_target_pairs={{0,1},{1,2},{2,3},{3,4},{4,5},{5,6},{6,7},{8,9},{9,10},{10,11},{11... | collective-permute-start | bytes 1572872 | tf_op jit(solution)/shard_map/ppermute | solution.py:14
where the time goes:
time: 239 us
  waiting for transfers between devices  90.6 us (38%)
  blocking collectives  63.9 us (27%)
  starting transfers between devices  47.6 us (20%)
  other arithmetic  32.4 us (14%)
  between operations  2.75 us (1%)
    ppermute x2, waiting for transfers between devices, passed_along(): return lax.ppermute(block, axis, route)  84.7 us
    psum x1, blocking collectives, per_device(): squared = lax.psum(local_sum, ('seg', 'slab'))  63.9 us
    ppermute x4, starting transfers between devices, extended_2(): lax.ppermute(lax.slice_in_dim(block, block.shape[dim] - width, None, axis...  36 us
    add x2, other arithmetic, per_device(): state + 0.1 * (planar(extended) + rate * state * (1.0 - state) + source)  7.82 us
    ppermute x2, starting transfers between devices, passed_along(): return lax.ppermute(block, axis, route)  6.08 us
    reduce_sum x1, other arithmetic, per_device(): jnp.sum(grad_control * grad_control) + jnp.sum(grad_start * grad_start)  6.06 us
    broadcast_in_dim x1, other arithmetic, per_device(): (source - scale * grad_control)[None]  5.91 us
    ppermute x4, waiting for transfers between devices, extended_2(): lax.ppermute(lax.slice_in_dim(block, block.shape[dim] - width, None, axis...  5.9 us
  transfers between devices with their start and end apart: 10, of which 6 were waited for; matrix products, arithmetic and copies ran while one was open for 0% of the time, Pallas kernels for 0%

commit v1 on v0

v1 whole, which is shorter than its diff:
```python
import functools

import jax
import jax.numpy as jnp
from jax import lax
from jax.experimental import pallas as pl
from jax.experimental.pallas import tpu as pltpu
from jax.sharding import PartitionSpec as P

CHUNKS = 8
TILE = 16
PAD = 8
LAG_U = 3
LAG_1 = 1
LAG_0 = 2
LAG_S = 3
MESH = pl.DeviceIdType.MESH


def kernel(
    n_seg, n_slab,
    cp, ctl_in, rate_in, target,
    gs_out, gc_out, tot_out,
    u0, u1, l2, l1, ctl, rat, end, cpn, prior, gs, gc, acc, slot_a, slot_b,
    sem_u0, sem_ctl, sem_rat, sem_alt_c, sem_alt_p, sem_gs, sem_gc,
    hs, hr, zs, zr, as_, ar, bs, br,
):
    me_seg = lax.axis_index("seg")
    me_slab = lax.axis_index("slab")
    layers, rows, cols = cp.shape[1:]
    size = rows // CHUNKS
    tiles = size // TILE
    top = layers + 1
    has_low = me_slab > 0
    has_high = me_slab < n_slab - 1
    first = me_seg == 0
    last = me_seg == n_seg - 1

    def span(c):
        return pl.ds(pl.multiple_of(c * size, size), size)

    def padded(c):
        return pl.ds(pl.multiple_of(c * size + PAD, 8), size)

    def load_u0(c):
        return pltpu.make_async_copy(
            cp.at[0, :, span(c)], u0.at[pl.ds(1, layers), padded(c)], sem_u0.at[c])

    def load_ctl(c):
        return pltpu.make_async_copy(ctl_in.at[0, :, span(c)], ctl.at[:, span(c)], sem_ctl.at[c])

    def load_rat(c):
        return pltpu.make_async_copy(rate_in.at[:, span(c)], rat.at[:, span(c)], sem_rat.at[c])

    def alt_c(c):
        return pltpu.make_async_copy(target.at[:, span(c)], cpn.at[:, span(c)], sem_alt_c.at[c])

    def alt_p(c):
        return pltpu.make_async_copy(cp.at[0, :, span(c)], prior.at[:, span(c)], sem_alt_p.at[c])

    def save_gs(c):
        return pltpu.make_async_copy(gs.at[:, span(c)], gs_out.at[:, span(c)], sem_gs.at[c])

    def save_gc(c):
        return pltpu.make_async_copy(gc.at[:, span(c)], gc_out.at[:, span(c)], sem_gc.at[c])

    def halo_down(k, buf, c):
        src = cp.at[0, 0, span(c)] if buf is u0 else buf.at[1, padded(c)]
        return pltpu.make_async_remote_copy(
            src, buf.at[top, padded(c)], hs.at[k, 0, c], hr.at[k, 0, c],
            device_id={"slab": me_slab - 1}, device_id_type=MESH)

    def halo_up(k, buf, c):
        src = cp.at[0, layers - 1, span(c)] if buf is u0 else buf.at[layers, padded(c)]
        return pltpu.make_async_remote_copy(
            src, buf.at[0, padded(c)], hs.at[k, 1, c], hr.at[k, 1, c],
            device_id={"slab": me_slab + 1}, device_id_type=MESH)

    def send_halo(k, buf, c):
        @pl.when(has_low)
        def _():
            halo_down(k, buf, c).start()

        @pl.when(has_high)
        def _():
            halo_up(k, buf, c).start()

    def wait_halo(k, buf, c):
        @pl.when(has_high)
        def _():
            halo_down(k, buf, c).wait_recv()

        @pl.when(has_low)
        def _():
            halo_up(k, buf, c).wait_recv()

    def send_cp(c):
        return pltpu.make_async_remote_copy(
            cp.at[0, :, span(c)], cpn.at[:, span(c)], zs.at[0, c], zr.at[0, c],
            device_id={"seg": me_seg - 1}, device_id_type=MESH)

    def send_end(c):
        return pltpu.make_async_remote_copy(
            end.at[:, span(c)], prior.at[:, span(c)], zs.at[1, c], zr.at[1, c],
            device_id={"seg": me_seg + 1}, device_id_type=MESH)

    barrier = pltpu.get_barrier_semaphore()
    for d in range(1, n_slab):
        pl.semaphore_signal(
            barrier, inc=1, device_id={"slab": lax.rem(me_slab + d, n_slab)}, device_id_type=MESH)
    for d in range(1, n_seg):
        pl.semaphore_signal(
            barrier, inc=1, device_id={"seg": lax.rem(me_seg + d, n_seg)}, device_id_type=MESH)

    @pl.loop(0, CHUNKS)
    def _(c):
        load_u0(c).start()
        load_ctl(c).start()
        load_rat(c).start()

    edge = jnp.zeros((PAD, cols), jnp.float32)
    for buf in (u0, u1, l2, l1):
        for z in range(1, top):
            buf[z, pl.ds(0, PAD), :] = edge
            buf[z, pl.ds(rows + PAD, PAD), :] = edge

    def clear(z):
        @pl.loop(0, rows // PAD)
        def _(i):
            for buf in (u0, u1, l2, l1):
                buf[z, pl.ds(pl.multiple_of(i * PAD + PAD, 8), PAD), :] = edge

    @pl.when(jnp.logical_not(has_low))
    def _():
        clear(0)

    @pl.when(jnp.logical_not(has_high))
    def _():
        clear(top)

    acc[...] = jnp.zeros_like(acc)
    pl.semaphore_wait(barrier, n_slab - 1 + n_seg - 1)

    @pl.loop(0, CHUNKS)
    def _(c):
        send_halo(0, u0, c)

        @pl.when(jnp.logical_not(first))
        def _():
            send_cp(c).start()

    @pl.loop(0, CHUNKS)
    def _(c):
        @pl.when(last)
        def _():
            alt_c(c).start()

        @pl.when(first)
        def _():
            alt_p(c).start()

    lane = lax.broadcasted_iota(jnp.int32, (TILE, cols), 1)
    at_left = lane == 0
    at_right = lane == cols - 1

    def laplace(buf, z, r):
        tall = buf[z, pl.ds(pl.multiple_of(r - PAD, 8), TILE + 2 * PAD), :]
        mid = tall[PAD:PAD + TILE]
        beside = buf[z + 1, pl.ds(r, TILE), :] + buf[z - 1, pl.ds(r, TILE), :]
        beside = beside + (tall[PAD + 1:PAD + 1 + TILE] + tall[PAD - 1:PAD - 1 + TILE])
        right = jnp.where(at_right, 0.0, pltpu.roll(mid, cols - 1, 1))
        left = jnp.where(at_left, 0.0, pltpu.roll(mid, 1, 1))
        return mid, beside + (right + left) - 6.0 * mid

    def each_tile(c, body):
        @pl.loop(0, tiles)
        def _(i):
            r = pl.multiple_of(c * size + i * TILE, 8)
            for z in range(layers):
                body(z, r, pl.ds(r, TILE), pl.multiple_of(r + PAD, 8))

    def add_square(v):
        sq = v * v
        part = sq[:PAD]
        for i in range(1, TILE // PAD):
            part = part + sq[i * PAD:(i + 1) * PAD]
        acc[...] = acc[...] + part

    def forward(src, c, dst):
        def body(z, r, at, p):
            u, lap = laplace(src, z + 1, p)
            new = u + 0.1 * (lap + rat[z, at, :] * u * (1.0 - u) + ctl[z, at, :])
            if dst is u1:
                u1[z + 1, pl.ds(p, TILE), :] = new
            else:
                end[z, at, :] = new
        each_tile(c, body)

    load_u0(0).wait()

    @pl.loop(0, CHUNKS + LAG_U)
    def _(i):
        @pl.when(i < CHUNKS)
        def _():
            @pl.when(i < CHUNKS - 1)
            def _():
                load_u0(i + 1).wait()
            load_ctl(i).wait()
            load_rat(i).wait()
            wait_halo(0, u0, i)
            forward(u0, i, u1)
            send_halo(1, u1, i)

        @pl.when(i >= LAG_U)
        def _():
            c = i - LAG_U
            wait_halo(1, u1, c)
            forward(u1, c, end)

            @pl.when(jnp.logical_not(last))
            def _():
                send_end(c).start()

    def do_defect(c):
        @pl.when(last)
        def _():
            alt_c(c).wait()

        @pl.when(jnp.logical_not(last))
        def _():
            send_cp(c).wait_recv()

        def body(z, r, at, p):
            l2[z + 1, pl.ds(p, TILE), :] = end[z, at, :] - cpn[z, at, :]
        each_tile(c, body)
        send_halo(2, l2, c)

    def do_l1(c):
        wait_halo(2, l2, c)

        def body(z, r, at, p):
            lam, lap = laplace(l2, z + 1, p)
            new = lam + 0.1 * (lap + rat[z, at, :] * (1.0 - 2.0 * u1[z + 1, pl.ds(p, TILE), :]) * lam)
            l1[z + 1, pl.ds(p, TILE), :] = new
            g = 0.1 * (lam + new)
            gc[z, at, :] = g
            add_square(g)
        each_tile(c, body)
        send_halo(3, l1, c)
        save_gc(c).start()

    def do_l0(c):
        wait_halo(3, l1, c)

        def body(z, r, at, p):
            lam, lap = laplace(l1, z + 1, p)
            start = u0[z + 1, pl.ds(p, TILE), :]
            gs[z, at, :] = lam + 0.1 * (lap + rat[z, at, :] * (1.0 - 2.0 * start) * lam)
        each_tile(c, body)

    def do_start(c):
        @pl.when(first)
        def _():
            alt_p(c).wait()

        @pl.when(jnp.logical_not(first))
        def _():
            send_end(c).wait_recv()

        def body(z, r, at, p):
            g = gs[z, at, :] - (prior[z, at, :] - u0[z + 1, pl.ds(p, TILE), :])
            gs[z, at, :] = g
            add_square(g)
        each_tile(c, body)
        save_gs(c).start()

    @pl.loop(0, CHUNKS + LAG_S)
    def _(i):
        @pl.when(i < CHUNKS)
        def _():
            do_defect(i)

        @pl.when(jnp.logical_and(i >= LAG_1, i < CHUNKS + LAG_1))
        def _():
            do_l1(i - LAG_1)

        @pl.when(jnp.logical_and(i >= LAG_0, i < CHUNKS + LAG_0))
        def _():
            do_l0(i - LAG_0)

        @pl.when(i >= LAG_S)
        def _():
            do_start(i - LAG_S)

    tile = acc[:, :128]
    for j in range(1, cols // 128):
        tile = tile + acc[:, j * 128:(j + 1) * 128]

    def total(value, slots, axis, me, count, ss, sr):
        def copy(d, owner, device):
            return pltpu.make_async_remote_copy(
                slots.at[owner], slots.at[owner], ss.at[d], sr.at[owner],
                device_id={axis: device}, device_id_type=MESH)

        slots[me] = value
        for d in range(1, count):
            copy(d, me, lax.rem(me + d, count)).start()
        for d in range(1, count):
            source = lax.rem(me + count - d, count)
            copy(d, source, source).wait_recv()
        result = slots[0]
        for j in range(1, count):
            result = result + slots[j]
        for d in range(1, count):
            copy(d, me, lax.rem(me + d, count)).wait_send()
        return result

    tile = total(tile, slot_a, "slab", me_slab, n_slab, as_, ar)
    tile = total(tile, slot_b, "seg", me_seg, n_seg, bs, br)
    tot_out[...] = tile

    @pl.loop(0, CHUNKS)
    def _(c):
        save_gs(c).wait()
        save_gc(c).wait()
        for k, buf in enumerate((u0, u1, l2, l1)):
            @pl.when(has_low)
            def _():
                halo_down(k, buf, c).wait_send()

            @pl.when(has_high)
            def _():
                halo_up(k, buf, c).wait_send()

        @pl.when(jnp.logical_not(first))
        def _():
            send_cp(c).wait_send()

        @pl.when(jnp.logical_not(last))
        def _():
            send_end(c).wait_send()


def per_device(checkpoints, control, rate, target):
    n_seg = lax.axis_size("seg")
    n_slab = lax.axis_size("slab")
    layers, rows, cols = rate.shape
    f32 = jnp.float32
    block = pltpu.VMEM((layers, rows, cols), f32)
    wide = pltpu.VMEM((layers + 2, rows + 2 * PAD, cols), f32)
    dma = pltpu.SemaphoreType.DMA
    anywhere = pl.BlockSpec(memory_space=pl.ANY)
    gs, gc, tot = pl.pallas_call(
        functools.partial(kernel, n_seg, n_slab),
        out_shape=(
            jax.ShapeDtypeStruct((layers, rows, cols), f32),
            jax.ShapeDtypeStruct((layers, rows, cols), f32),
            jax.ShapeDtypeStruct((8, 128), f32),
        ),
        in_specs=[anywhere] * 4,
        out_specs=(anywhere, anywhere, pl.BlockSpec(memory_space=pltpu.VMEM)),
        scratch_shapes=[
            wide, wide, wide, wide,
            block, block, block, block, block, block, block,
            pltpu.VMEM((PAD, cols), f32),
            pltpu.VMEM((n_slab, 8, 128), f32),
            pltpu.VMEM((n_seg, 8, 128), f32),
            dma((CHUNKS,)), dma((CHUNKS,)), dma((CHUNKS,)),
            dma((CHUNKS,)), dma((CHUNKS,)), dma((CHUNKS,)), dma((CHUNKS,)),
            dma((4, 2, CHUNKS)), dma((4, 2, CHUNKS)),
            dma((2, CHUNKS)), dma((2, CHUNKS)),
            dma((n_slab,)), dma((n_slab,)),
            dma((n_seg,)), dma((n_seg,)),
        ],
        compiler_params=pltpu.CompilerParams(
            collective_id=0, has_side_effects=True, vmem_limit_bytes=58 << 20
        ),
        name="shooting",
    )(checkpoints, control, rate, target)
    count = 2.0 * n_seg * n_slab * rate.size
    scale = 0.5 / jnp.sqrt(jnp.sum(tot) / count + 1e-06)
    return checkpoints - scale * gs[None], control - scale * gc[None]


def solution(mesh):
    return jax.shard_map(
        per_device,
        mesh=mesh,
        in_specs=(
            P("seg", "slab", None, None),
            P("seg", "slab", None, None),
            P("slab", None, None),
            P("slab", None, None),
        ),
        out_specs=(P("seg", "slab", None, None), P("seg", "slab", None, None)),
        check_vma=False,
    )
```

time: 239 us -> 79.4 us (0.33)
  waiting for transfers between devices: 90.6 us -> 0 us
  Pallas kernels: 0 us -> 70.7 us
  blocking collectives: 63.9 us -> 0 us
  starting transfers between devices: 47.6 us -> 0 us
  other arithmetic: 32.4 us -> 7.18 us
    ppermute x10 -> x0, waiting for transfers between devices: 90.6 us -> none  [the longest x2 84.7 us: passed_along(): return lax.ppermute(block, axis, route)]
    pallas_call x0 -> x1, Pallas kernels: none -> 70.7 us  [per_device(): pl.pallas_call(functools.partial(kernel, n_seg, n_slab), out_shape=(jax.S...]
    psum x1 -> x0, blocking collectives: 63.9 us -> none  [per_device(): squared = lax.psum(local_sum, ('seg', 'slab'))]
    ppermute x10 -> x0, starting transfers between devices: 47.6 us -> none  [the longest x4 36 us: extended_2(): lax.ppermute(lax.slice_in_dim(block, block.shape[dim] - width, None, axis...]
    reduce_sum x2 -> x1, other arithmetic: 11.5 us -> 1.28 us  [per_device(): scale = 0.5 / jnp.sqrt(jnp.sum(tot) / count + 1e-06)]
    add x2 -> x0, other arithmetic: 7.82 us -> none  [per_device(): state + 0.1 * (planar(extended) + rate * state * (1.0 - state) + source)]
    select_n x2 -> x0, other arithmetic: 7.19 us -> none  [the longest x1 3.78 us: per_device(): defect = jnp.where(is_last, state - target, returned)]
    broadcast_in_dim x1 -> x0, other arithmetic: 5.91 us -> none  [per_device(): (source - scale * grad_control)[None]]
  transfers between devices with their start and end apart: 10 -> 0, of which waited for: 6 -> 0; matrix products, arithmetic and copies ran while one was open for 0% -> 0% of each run, Pallas kernels for 0% -> 0%
where the time goes in v1:
time: 79.4 us; the launch traced here: 79.2 us
  Pallas kernels  70.7 us (89%)
  other arithmetic  7.18 us (9%)
  between operations  1.35 us (2%)
    pallas_call x1, Pallas kernels, per_device(): pl.pallas_call(functools.partial(kernel, n_seg, n_slab), out_shape=(jax.S...  70.7 us
    sub x1, other arithmetic, per_device(): return (checkpoints - scale * gs[None], control - scale * gc[None])  5.9 us

profile of v1, /device:TPU:0, one launch (start us, length us, event | category | flops | bytes accessed | tf_op | source)
XLA Modules:
  0.0 79.2 jit_solution(8666741172502332918)
XLA Ops:
  0.6 0.0 copy-start
  0.6 70.7 %shooting.1 = (f32[4,256,512]{2,1,0:T(8,128)}, f32[4,256,512]{2,1,0:T(8,128)}, f32[8,128]{1,0:T(8,128)}) custom-call(f32[1,4,256,512]{3,2,1,0:T(8,128)} %cp.1, f32[1,4,256,512]{3,2,1,0:T(8,128)} %ctl_in.1, f32[4,256,512]{2,1,0:T(8,128)} %rate_in.1, f32[4,256,512]{2,1,0:T(8,128)} %target.1), custom_call_target="tpu_custom_call" | custom-call | tf_op jit(solution)/shard_map/shooting/pallas_call | solution.py:353
  71.3 1.3 %reduce_sum.9 = f32[]{:T(128)} reduce(f32[8,128]{1,0:T(8,128)} %get-tuple-element.5, f32[]{:T(128)} %constant.2.clone.1), dimensions={0,1}, to_apply=%region_0.0 | reduce | flops 1023 | bytes 4104 | tf_op jit(solution)/shard_map/reduce_sum | solution.py:381
  73.3 0.0 copy-done
  73.3 5.9 %bitcast_subtract_fusion = (f32[1,4,256,512]{3,2,1,0:T(8,128)}, f32[1,4,256,512]{3,2,1,0:T(8,128)}) fusion(f32[1,4,256,512]{3,2,1,0:T(8,128)S(1)} %copy-done, f32[4,256,512]{2,1,0:T(8,128)} %get-tuple-element.7, f32[]{:T(128)S(6)} %div.7, f32[1,4,256,512]{3,2,1,0:T(8,128)} %cp.1, f32[4,256,512]{2,1,0:T(8,128)} %get-tuple-element.6), kind=kLoop, calls=%fused_computation | loop fusion | flops 2097152 | bytes 12582916 | tf_op jit(solution)/shard_map/sub | solution.py:382
Async XLA Ops:
  0.6 72.6 %copy-start = (f32[1,4,256,512]{3,2,1,0:T(8,128)S(1)}, f32[1,4,256,512]{3,2,1,0:T(8,128)}, u32[]{:S(2)}) copy-start(f32[1,4,256,512]{3,2,1,0:T(8,128)} %ctl_in.1) | copy-start | bytes 6291460

commit v2 on v1

--- a/solution.py
+++ b/solution.py
@@ -8,9 +8,11 @@
 from jax.sharding import PartitionSpec as P
 
 CHUNKS = 8
+PARTS = 8
 TILE = 16
 PAD = 8
-LAG_U = 3
+LAG_U = 2
+AHEAD = 3
 LAG_1 = 1
 LAG_0 = 2
 LAG_S = 3
@@ -20,9 +22,9 @@
 def kernel(
     n_seg, n_slab,
     cp, ctl_in, rate_in, target,
-    gs_out, gc_out, tot_out,
-    u0, u1, l2, l1, ctl, rat, end, cpn, prior, gs, gc, acc, slot_a, slot_b,
-    sem_u0, sem_ctl, sem_rat, sem_alt_c, sem_alt_p, sem_gs, sem_gc,
+    u0, ctl, gs, gc, tot_out,
+    u1, l2, l1, rat, end, cpn, prior, acc, slot_a, slot_b,
+    sem_u0, sem_ctl, sem_rat, sem_alt_c, sem_alt_p,
     hs, hr, zs, zr, as_, ar, bs, br,
 ):
     me_seg = lax.axis_index("seg")
@@ -58,12 +60,6 @@
     def alt_p(c):
         return pltpu.make_async_copy(cp.at[0, :, span(c)], prior.at[:, span(c)], sem_alt_p.at[c])
 
-    def save_gs(c):
-        return pltpu.make_async_copy(gs.at[:, span(c)], gs_out.at[:, span(c)], sem_gs.at[c])
-
-    def save_gc(c):
-        return pltpu.make_async_copy(gc.at[:, span(c)], gc_out.at[:, span(c)], sem_gc.at[c])
-
     def halo_down(k, buf, c):
         src = cp.at[0, 0, span(c)] if buf is u0 else buf.at[1, padded(c)]
         return pltpu.make_async_remote_copy(
@@ -141,10 +137,11 @@
     acc[...] = jnp.zeros_like(acc)
     pl.semaphore_wait(barrier, n_slab - 1 + n_seg - 1)
 
+    for c in range(AHEAD):
+        send_halo(0, u0, c)
+
     @pl.loop(0, CHUNKS)
     def _(c):
-        send_halo(0, u0, c)
-
         @pl.when(jnp.logical_not(first))
         def _():
             send_cp(c).start()
@@ -207,6 +204,10 @@
                 load_u0(i + 1).wait()
             load_ctl(i).wait()
             load_rat(i).wait()
+
+            @pl.when(i < CHUNKS - AHEAD)
+            def _():
+                send_halo(0, u0, i + AHEAD)
             wait_halo(0, u0, i)
             forward(u0, i, u1)
             send_halo(1, u1, i)
@@ -247,7 +248,6 @@
             add_square(g)
         each_tile(c, body)
         send_halo(3, l1, c)
-        save_gc(c).start()
 
     def do_l0(c):
         wait_halo(3, l1, c)
@@ -272,7 +272,6 @@
             gs[z, at, :] = g
             add_square(g)
         each_tile(c, body)
-        save_gs(c).start()
 
     @pl.loop(0, CHUNKS + LAG_S)
     def _(i):
@@ -311,18 +310,18 @@
         result = slots[0]
         for j in range(1, count):
             result = result + slots[j]
-        for d in range(1, count):
-            copy(d, me, lax.rem(me + d, count)).wait_send()
+        sent.extend(copy(d, me, lax.rem(me + d, count)) for d in range(1, count))
         return result
 
+    sent = []
     tile = total(tile, slot_a, "slab", me_slab, n_slab, as_, ar)
     tile = total(tile, slot_b, "seg", me_seg, n_seg, bs, br)
     tot_out[...] = tile
+    for copy in sent:
+        copy.wait_send()
 
     @pl.loop(0, CHUNKS)
     def _(c):
-        save_gs(c).wait()
-        save_gc(c).wait()
         for k, buf in enumerate((u0, u1, l2, l1)):
             @pl.when(has_low)
             def _():
@@ -339,6 +338,40 @@
         @pl.when(jnp.logical_not(last))
         def _():
             send_end(c).wait_send()
+
+
+def update_kernel(
+    count, u0, ctl, gs, gc, tot, new_cp, new_ctl, out_a, out_b, sem_a, sem_b
+):
+    layers, rows, cols = ctl.shape
+    size = rows // PARTS
+    sum_of = jnp.sum(jnp.sum(tot[...], axis=0, keepdims=True), axis=1, keepdims=True)
+    scale = jnp.broadcast_to(0.5 / jnp.sqrt(sum_of / count + 1e-06), (PAD, cols))
+
+    def save(c):
+        at = pl.ds(pl.multiple_of(c * size, size), size)
+        return (
+            pltpu.make_async_copy(out_a.at[:, at], new_cp.at[0, :, at], sem_a.at[c]),
+            pltpu.make_async_copy(out_b.at[:, at], new_ctl.at[0, :, at], sem_b.at[c]),
+        )
+
+    @pl.loop(0, PARTS)
+    def _(c):
+        @pl.loop(0, size // PAD)
+        def _(i):
+            r = pl.multiple_of(c * size + i * PAD, 8)
+            at = pl.ds(r, PAD)
+            for z in range(layers):
+                start = u0[z + 1, pl.ds(pl.multiple_of(r + PAD, 8), PAD), :]
+                out_a[z, at, :] = start - scale * gs[z, at, :]
+                out_b[z, at, :] = ctl[z, at, :] - scale * gc[z, at, :]
+        for copy in save(c):
+            copy.start()
+
+    @pl.loop(0, PARTS)
+    def _(c):
+        for copy in save(c):
+            copy.wait()
 
 
 def per_device(checkpoints, control, rate, target):
@@ -349,37 +382,44 @@
     block = pltpu.VMEM((layers, rows, cols), f32)
     wide = pltpu.VMEM((layers + 2, rows + 2 * PAD, cols), f32)
     dma = pltpu.SemaphoreType.DMA
-    anywhere = pl.BlockSpec(memory_space=pl.ANY)
-    gs, gc, tot = pl.pallas_call(
+    hbm = pl.BlockSpec(memory_space=pltpu.HBM)
+    vmem = pl.BlockSpec(memory_space=pltpu.VMEM)
+    kept = pl.pallas_call(
         functools.partial(kernel, n_seg, n_slab),
-        out_shape=(
-            jax.ShapeDtypeStruct((layers, rows, cols), f32),
-            jax.ShapeDtypeStruct((layers, rows, cols), f32),
-            jax.ShapeDtypeStruct((8, 128), f32),
-        ),
-        in_specs=[anywhere] * 4,
-        out_specs=(anywhere, anywhere, pl.BlockSpec(memory_space=pltpu.VMEM)),
+        out_shape=(wide, block, block, block, pltpu.VMEM((8, 128), f32)),
+        in_specs=[hbm] * 4,
+        out_specs=(vmem,) * 5,
         scratch_shapes=[
-            wide, wide, wide, wide,
-            block, block, block, block, block, block, block,
+            wide, wide, wide,
+            block, block, block, block,
             pltpu.VMEM((PAD, cols), f32),
             pltpu.VMEM((n_slab, 8, 128), f32),
             pltpu.VMEM((n_seg, 8, 128), f32),
             dma((CHUNKS,)), dma((CHUNKS,)), dma((CHUNKS,)),
-            dma((CHUNKS,)), dma((CHUNKS,)), dma((CHUNKS,)), dma((CHUNKS,)),
+            dma((CHUNKS,)), dma((CHUNKS,)),
             dma((4, 2, CHUNKS)), dma((4, 2, CHUNKS)),
             dma((2, CHUNKS)), dma((2, CHUNKS)),
             dma((n_slab,)), dma((n_slab,)),
             dma((n_seg,)), dma((n_seg,)),
         ],
         compiler_params=pltpu.CompilerParams(
-            collective_id=0, has_side_effects=True, vmem_limit_bytes=58 << 20
+            collective_id=0, has_side_effects=True, vmem_limit_bytes=50 << 20
         ),
         name="shooting",
     )(checkpoints, control, rate, target)
     count = 2.0 * n_seg * n_slab * rate.size
-    scale = 0.5 / jnp.sqrt(jnp.sum(tot) / count + 1e-06)
-    return checkpoints - scale * gs[None], control - scale * gc[None]
+    return pl.pallas_call(
+        functools.partial(update_kernel, count),
+        out_shape=(
+            jax.ShapeDtypeStruct(checkpoints.shape, f32),
+            jax.ShapeDtypeStruct(control.shape, f32),
+        ),
+        in_specs=[vmem] * 5,
+        out_specs=(hbm, hbm),
+        scratch_shapes=[block, block, dma((PARTS,)), dma((PARTS,))],
+        compiler_params=pltpu.CompilerParams(vmem_limit_bytes=8 << 20),
+        name="update",
+    )(*kept)
 
 
 def solution(mesh):

time: 79.4 us -> 71.1 us (0.90)
  other arithmetic: 7.18 us -> 0 us
    sub x1 -> x0, other arithmetic: 5.9 us -> none  [per_device(): return (checkpoints - scale * gs[None], control - scale * gc[None])]
    reduce_sum x1 -> x0, other arithmetic: 1.28 us -> none  [per_device(): scale = 0.5 / jnp.sqrt(jnp.sum(tot) / count + 1e-06)]
    pallas_call x1 -> x2, Pallas kernels: 70.7 us -> 70.3 us  [the longest x1 68 us: per_device(): pl.pallas_call(functools.partial(kernel, n_seg, n_slab), out_shape=(wide,...]
where the time goes in v2:
time: 71.1 us; the launch traced here: 71 us
  Pallas kernels  70.3 us (99%)
    pallas_call x1, Pallas kernels, per_device(): pl.pallas_call(functools.partial(kernel, n_seg, n_slab), out_shape=(wide,...  68 us
    pallas_call x1, Pallas kernels, per_device(): pl.pallas_call(functools.partial(update_kernel, count), out_shape=(jax.Sh...  2.3 us

profile of v2, /device:TPU:0, one launch (start us, length us, event | category | flops | bytes accessed | tf_op | source)
XLA Modules:
  0.0 71.0 jit_solution(7897222514006121506)
XLA Ops:
  0.6 68.0 %shooting.1 = (f32[6,272,512]{2,1,0:T(8,128)S(1)}, f32[4,256,512]{2,1,0:T(8,128)S(1)}, f32[4,256,512]{2,1,0:T(8,128)S(1)}, f32[4,256,512]{2,1,0:T(8,128)S(1)}, f32[8,128]{1,0:T(8,128)S(1)}) custom-call(f32[1,4,256,512]{3,2,1,0:T(8,128)} %cp.1, f32[1,4,256,512]{3,2,1,0:T(8,128)} %ctl_in.1, f32[4,256,512]{2,1,0:T(8,128)} %rate_in.1, f32[4,256,512]{2,1,0:T(8,128)} %target.1), custom_call_target="tpu_custom_call" | custom-call | tf_op jit(solution)/shard_map/shooting/pallas_call | solution.py:387
  68.7 2.3 %update.1 = (f32[1,4,256,512]{3,2,1,0:T(8,128)}, f32[1,4,256,512]{3,2,1,0:T(8,128)}) custom-call(f32[6,272,512]{2,1,0:T(8,128)S(1)} %get-tuple-element.7.u0, f32[4,256,512]{2,1,0:T(8,128)S(1)} %get-tuple-element.8.ctl, f32[4,256,512]{2,1,0:T(8,128)S(1)} %get-tuple-element.9.gs, f32[4,256,512]{2,1,0:T(8,128)S(1)} %get-tuple-element.10.gc, ...), custom_call_target="tpu_custom_call" | custom-call | tf_op jit(solution)/shard_map/update/pallas_call | solution.py:411

commit v3 on v2

--- a/solution.py
+++ b/solution.py
@@ -13,7 +13,6 @@
 PAD = 8
 LAG_U = 2
 AHEAD = 3
-LAG_1 = 1
 LAG_0 = 2
 LAG_S = 3
 MESH = pl.DeviceIdType.MESH
@@ -90,23 +89,33 @@
         def _():
             halo_up(k, buf, c).wait_recv()
 
-    def send_cp(c):
+    inner = range(1, layers - 1)
+    rim = (0, layers - 1)
+    parts = (pl.ds(1, layers - 2), 0, layers - 1)
+
+    def send_cp(c, part):
+        at = parts[part]
         return pltpu.make_async_remote_copy(
-            cp.at[0, :, span(c)], cpn.at[:, span(c)], zs.at[0, c], zr.at[0, c],
+            cp.at[0, at, span(c)], cpn.at[at, span(c)], zs.at[part + 3, c], zr.at[part + 3, c],
             device_id={"seg": me_seg - 1}, device_id_type=MESH)
 
-    def send_end(c):
+    def send_end(c, part):
+        at = parts[part]
         return pltpu.make_async_remote_copy(
-            end.at[:, span(c)], prior.at[:, span(c)], zs.at[1, c], zr.at[1, c],
+            end.at[at, span(c)], prior.at[at, span(c)], zs.at[part, c], zr.at[part, c],
             device_id={"seg": me_seg + 1}, device_id_type=MESH)
 
     barrier = pltpu.get_barrier_semaphore()
-    for d in range(1, n_slab):
-        pl.semaphore_signal(
-            barrier, inc=1, device_id={"slab": lax.rem(me_slab + d, n_slab)}, device_id_type=MESH)
-    for d in range(1, n_seg):
-        pl.semaphore_signal(
-            barrier, inc=1, device_id={"seg": lax.rem(me_seg + d, n_seg)}, device_id_type=MESH)
+    slab_peers = [{"slab": lax.rem(me_slab + d, n_slab)} for d in range(1, n_slab)]
+    seg_peers = [{"seg": lax.rem(me_seg + d, n_seg)} for d in range(1, n_seg)]
+    both = [
+        {"seg": lax.rem(me_seg + e, n_seg), "slab": lax.rem(me_slab + d, n_slab)}
+        for e in range(1, n_seg) for d in range(1, n_slab)
+    ]
+    direct = n_seg * n_slab <= 32
+    peers = slab_peers + seg_peers + (both if direct else [])
+    for peer in peers:
+        pl.semaphore_signal(barrier, inc=1, device_id=peer, device_id_type=MESH)
 
     @pl.loop(0, CHUNKS)
     def _(c):
@@ -135,16 +144,21 @@
         clear(top)
 
     acc[...] = jnp.zeros_like(acc)
-    pl.semaphore_wait(barrier, n_slab - 1 + n_seg - 1)
+    pl.semaphore_wait(barrier, len(peers))
 
     for c in range(AHEAD):
         send_halo(0, u0, c)
 
-    @pl.loop(0, CHUNKS)
-    def _(c):
-        @pl.when(jnp.logical_not(first))
-        def _():
-            send_cp(c).start()
+    @pl.when(jnp.logical_not(first))
+    def _():
+        @pl.loop(0, CHUNKS)
+        def _(c):
+            send_cp(c, 1).start()
+            send_cp(c, 2).start()
+
+        @pl.loop(0, CHUNKS)
+        def _(c):
+            send_cp(c, 0).start()
 
     @pl.loop(0, CHUNKS)
     def _(c):
@@ -169,11 +183,11 @@
         left = jnp.where(at_left, 0.0, pltpu.roll(mid, 1, 1))
         return mid, beside + (right + left) - 6.0 * mid
 
-    def each_tile(c, body):
+    def each_tile(c, body, zs=range(layers)):
         @pl.loop(0, tiles)
         def _(i):
             r = pl.multiple_of(c * size + i * TILE, 8)
-            for z in range(layers):
+            for z in zs:
                 body(z, r, pl.ds(r, TILE), pl.multiple_of(r + PAD, 8))
 
     def add_square(v):
@@ -183,7 +197,7 @@
             part = part + sq[i * PAD:(i + 1) * PAD]
         acc[...] = acc[...] + part
 
-    def forward(src, c, dst):
+    def forward(src, c, dst, zs):
         def body(z, r, at, p):
             u, lap = laplace(src, z + 1, p)
             new = u + 0.1 * (lap + rat[z, at, :] * u * (1.0 - u) + ctl[z, at, :])
@@ -191,7 +205,7 @@
                 u1[z + 1, pl.ds(p, TILE), :] = new
             else:
                 end[z, at, :] = new
-        each_tile(c, body)
+        each_tile(c, body, zs)
 
     load_u0(0).wait()
 
@@ -209,32 +223,52 @@
             def _():
                 send_halo(0, u0, i + AHEAD)
             wait_halo(0, u0, i)
-            forward(u0, i, u1)
+            forward(u0, i, u1, range(layers))
             send_halo(1, u1, i)
+
+        @pl.when(jnp.logical_and(i >= 1, i <= CHUNKS))
+        def _():
+            c = i - 1
+            forward(u1, c, end, inner)
+
+            @pl.when(jnp.logical_not(last))
+            def _():
+                send_end(c, 0).start()
 
         @pl.when(i >= LAG_U)
         def _():
             c = i - LAG_U
             wait_halo(1, u1, c)
-            forward(u1, c, end)
+            forward(u1, c, end, rim)
 
             @pl.when(jnp.logical_not(last))
             def _():
-                send_end(c).start()
-
-    def do_defect(c):
-        @pl.when(last)
-        def _():
-            alt_c(c).wait()
-
-        @pl.when(jnp.logical_not(last))
-        def _():
-            send_cp(c).wait_recv()
-
+                send_end(c, 1).start()
+                send_end(c, 2).start()
+
+    def defect(c, zs):
         def body(z, r, at, p):
             l2[z + 1, pl.ds(p, TILE), :] = end[z, at, :] - cpn[z, at, :]
-        each_tile(c, body)
+        each_tile(c, body, zs)
+
+    @pl.loop(0, CHUNKS)
+    def _(c):
+        @pl.when(last)
+        def _():
+            alt_c(c).wait()
+
+        @pl.when(jnp.logical_not(last))
+        def _():
+            send_cp(c, 1).wait_recv()
+            send_cp(c, 2).wait_recv()
+        defect(c, rim)
         send_halo(2, l2, c)
+
+    def do_defect(c):
+        @pl.when(jnp.logical_not(last))
+        def _():
+            send_cp(c, 0).wait_recv()
+        defect(c, inner)
 
     def do_l1(c):
         wait_halo(2, l2, c)
@@ -265,7 +299,8 @@
 
         @pl.when(jnp.logical_not(first))
         def _():
-            send_end(c).wait_recv()
+            for part in range(3):
+                send_end(c, part).wait_recv()
 
         def body(z, r, at, p):
             g = gs[z, at, :] - (prior[z, at, :] - u0[z + 1, pl.ds(p, TILE), :])
@@ -279,9 +314,13 @@
         def _():
             do_defect(i)
 
-        @pl.when(jnp.logical_and(i >= LAG_1, i < CHUNKS + LAG_1))
-        def _():
-            do_l1(i - LAG_1)
+        @pl.when(jnp.logical_and(i >= 1, i < CHUNKS))
+        def _():
+            do_l1(i - 1)
+
+        @pl.when(i == CHUNKS - 1)
+        def _():
+            do_l1(i)
 
         @pl.when(jnp.logical_and(i >= LAG_0, i < CHUNKS + LAG_0))
         def _():
@@ -295,30 +334,33 @@
     for j in range(1, cols // 128):
         tile = tile + acc[:, j * 128:(j + 1) * 128]
 
-    def total(value, slots, axis, me, count, ss, sr):
-        def copy(d, owner, device):
+    def total(value, slots, owner, peers, ss, sr):
+        count = len(peers)
+
+        def copy(at, peer):
             return pltpu.make_async_remote_copy(
-                slots.at[owner], slots.at[owner], ss.at[d], sr.at[owner],
-                device_id={axis: device}, device_id_type=MESH)
-
-        slots[me] = value
-        for d in range(1, count):
-            copy(d, me, lax.rem(me + d, count)).start()
-        for d in range(1, count):
-            source = lax.rem(me + count - d, count)
-            copy(d, source, source).wait_recv()
+                slots.at[at], slots.at[at], ss, sr, device_id=peer, device_id_type=MESH)
+
+        slots[owner] = value
+        for peer in peers:
+            copy(owner, peer).start()
+        everything = copy(pl.ds(0, count), peers[0])
+        everything.wait_recv()
         result = slots[0]
-        for j in range(1, count):
+        for j in range(1, count + 1):
             result = result + slots[j]
-        sent.extend(copy(d, me, lax.rem(me + d, count)) for d in range(1, count))
-        return result
-
-    sent = []
-    tile = total(tile, slot_a, "slab", me_slab, n_slab, as_, ar)
-    tile = total(tile, slot_b, "seg", me_seg, n_seg, bs, br)
+        return result, everything
+
+    if direct:
+        tile, sent_a = total(tile, slot_a, me_seg * n_slab + me_slab, peers, as_, ar)
+        sent = [sent_a]
+    else:
+        tile, sent_a = total(tile, slot_a, me_slab, slab_peers, as_, ar)
+        tile, sent_b = total(tile, slot_b, me_seg, seg_peers, bs, br)
+        sent = [sent_a, sent_b]
     tot_out[...] = tile
-    for copy in sent:
-        copy.wait_send()
+    for copies in sent:
+        copies.wait_send()
 
     @pl.loop(0, CHUNKS)
     def _(c):
@@ -333,11 +375,13 @@
 
         @pl.when(jnp.logical_not(first))
         def _():
-            send_cp(c).wait_send()
+            for part in range(3):
+                send_cp(c, part).wait_send()
 
         @pl.when(jnp.logical_not(last))
         def _():
-            send_end(c).wait_send()
+            for part in range(3):
+                send_end(c, part).wait_send()
 
 
 def update_kernel(
@@ -393,14 +437,13 @@
             wide, wide, wide,
             block, block, block, block,
             pltpu.VMEM((PAD, cols), f32),
-            pltpu.VMEM((n_slab, 8, 128), f32),
+            pltpu.VMEM((n_slab * n_seg, 8, 128), f32),
             pltpu.VMEM((n_seg, 8, 128), f32),
             dma((CHUNKS,)), dma((CHUNKS,)), dma((CHUNKS,)),
             dma((CHUNKS,)), dma((CHUNKS,)),
             dma((4, 2, CHUNKS)), dma((4, 2, CHUNKS)),
-            dma((2, CHUNKS)), dma((2, CHUNKS)),
-            dma((n_slab,)), dma((n_slab,)),
-            dma((n_seg,)), dma((n_seg,)),
+            dma((6, CHUNKS)), dma((6, CHUNKS)),
+            dma(()), dma(()), dma(()), dma(()),
         ],
         compiler_params=pltpu.CompilerParams(
             collective_id=0, has_side_effects=True, vmem_limit_bytes=50 << 20

time: 71.1 us -> 69.1 us (0.972)
  Pallas kernels: 70.3 us -> 68.4 us
    pallas_call x1, Pallas kernels: 68 us -> 66.1 us  [per_device(): pl.pallas_call(functools.partial(kernel, n_seg, n_slab), out_shape=(wide,...]
where the time goes in v3:
time: 69.1 us; the launch traced here: 69 us
  Pallas kernels  68.4 us (99%)
    pallas_call x1, Pallas kernels, per_device(): pl.pallas_call(functools.partial(kernel, n_seg, n_slab), out_shape=(wide,...  66.1 us
    pallas_call x1, Pallas kernels, per_device(): pl.pallas_call(functools.partial(update_kernel, count), out_shape=(jax.Sh...  2.3 us

profile of v3, /device:TPU:0, one launch (start us, length us, event | category | flops | bytes accessed | tf_op | source)
XLA Modules:
  0.0 69.0 jit_solution(15587557586318809287)
XLA Ops:
  0.6 66.1 %shooting.1 = (f32[6,272,512]{2,1,0:T(8,128)S(1)}, f32[4,256,512]{2,1,0:T(8,128)S(1)}, f32[4,256,512]{2,1,0:T(8,128)S(1)}, f32[4,256,512]{2,1,0:T(8,128)S(1)}, f32[8,128]{1,0:T(8,128)S(1)}) custom-call(f32[1,4,256,512]{3,2,1,0:T(8,128)} %cp.1, f32[1,4,256,512]{3,2,1,0:T(8,128)} %ctl_in.1, f32[4,256,512]{2,1,0:T(8,128)} %rate_in.1, f32[4,256,512]{2,1,0:T(8,128)} %target.1), custom_call_target="tpu_custom_call" | custom-call | tf_op jit(solution)/shard_map/shooting/pallas_call | solution.py:431
  66.7 2.3 %update.1 = (f32[1,4,256,512]{3,2,1,0:T(8,128)}, f32[1,4,256,512]{3,2,1,0:T(8,128)}) custom-call(f32[6,272,512]{2,1,0:T(8,128)S(1)} %get-tuple-element.7.u0, f32[4,256,512]{2,1,0:T(8,128)S(1)} %get-tuple-element.8.ctl, f32[4,256,512]{2,1,0:T(8,128)S(1)} %get-tuple-element.9.gs, f32[4,256,512]{2,1,0:T(8,128)S(1)} %get-tuple-element.10.gc, ...), custom_call_target="tpu_custom_call" | custom-call | tf_op jit(solution)/shard_map/update/pallas_call | solution.py:454

commit v4 on v3

--- a/solution.py
+++ b/solution.py
@@ -11,8 +11,8 @@
 PARTS = 8
 TILE = 16
 PAD = 8
-LAG_U = 2
-AHEAD = 3
+LAG_U = 4
+AHEAD = 8
 LAG_0 = 2
 LAG_S = 3
 MESH = pl.DeviceIdType.MESH

time: 69.1 us -> 68.7 us (level)
  no operation moved by 1% of the time
where the time goes in v4:
time: 68.7 us; the launch traced here: 68.6 us
  Pallas kernels  67.9 us (99%)
    pallas_call x1, Pallas kernels, per_device(): pl.pallas_call(functools.partial(kernel, n_seg, n_slab), out_shape=(wide,...  65.6 us
    pallas_call x1, Pallas kernels, per_device(): pl.pallas_call(functools.partial(update_kernel, count), out_shape=(jax.Sh...  2.3 us

profile of v4, /device:TPU:0, one launch (start us, length us, event | category | flops | bytes accessed | tf_op | source)
XLA Modules:
  0.0 68.6 jit_solution(2589345268884342140)
XLA Ops:
  0.6 65.6 %shooting.1 = (f32[6,272,512]{2,1,0:T(8,128)S(1)}, f32[4,256,512]{2,1,0:T(8,128)S(1)}, f32[4,256,512]{2,1,0:T(8,128)S(1)}, f32[4,256,512]{2,1,0:T(8,128)S(1)}, f32[8,128]{1,0:T(8,128)S(1)}) custom-call(f32[1,4,256,512]{3,2,1,0:T(8,128)} %cp.1, f32[1,4,256,512]{3,2,1,0:T(8,128)} %ctl_in.1, f32[4,256,512]{2,1,0:T(8,128)} %rate_in.1, f32[4,256,512]{2,1,0:T(8,128)} %target.1), custom_call_target="tpu_custom_call" | custom-call | tf_op jit(solution)/shard_map/shooting/pallas_call | solution.py:431
  66.3 2.3 %update.1 = (f32[1,4,256,512]{3,2,1,0:T(8,128)}, f32[1,4,256,512]{3,2,1,0:T(8,128)}) custom-call(f32[6,272,512]{2,1,0:T(8,128)S(1)} %get-tuple-element.7.u0, f32[4,256,512]{2,1,0:T(8,128)S(1)} %get-tuple-element.8.ctl, f32[4,256,512]{2,1,0:T(8,128)S(1)} %get-tuple-element.9.gs, f32[4,256,512]{2,1,0:T(8,128)S(1)} %get-tuple-element.10.gc, ...), custom_call_target="tpu_custom_call" | custom-call | tf_op jit(solution)/shard_map/update/pallas_call | solution.py:454
